TPU v7x, 32 devices: a whole 2x2x4 slice. The times are simulated.
32 devices in a mesh: group: 2 (over y), row: 8 (over z, x), col: 2 (over core).
Axes of the slice: x: 2, y: 2, z: 4, core: 2. Of those that a mesh axis runs over, the one named last changes fastest.
Arguments:
- map_in: bfloat16 [192, 96, 48], P(('group', 'row'), 'col'), parts along dimension 0, may hold values from -6 to 6
- embedding: bfloat16 [192, 96], P(('group', 'row')), parts along dimension 0, may hold values from -6 to 6
- w_row: bfloat16 [96, 48], replicated, may hold values from -0.625 to 0.625
- w_col: bfloat16 [96, 48], replicated, may hold values from -0.625 to 0.625
- first_kernel_weight: bfloat16 [3, 3, 48, 48], replicated, may hold values from -0.3125 to 0.3125
- first_bias: float32 [48], replicated, may hold values from -0.5 to 0.5
- second_kernel_weight: bfloat16 [3, 3, 48, 48], replicated, may hold values from -0.3125 to 0.3125
- second_bias: float32 [48], replicated, may hold values from -0.5 to 0.5
- w_mix: bfloat16 [48, 48], replicated, may hold values from -0.875 to 0.875
- b_mix: float32 [48], replicated, may hold values from -0.5 to 0.5
- w_head: float32 [48], replicated, may hold values from -0.875 to 0.875
Outputs:
- contacts: float32 [192, 96], P(('group', 'row'), 'col'), parts along dimension 0
There are 2 independent parts, one for each index of `group`. A program takes and returns all parts, laid end to end along the dimension named above; an argument that names none is the same for every part. Nothing has to cross between parts.
All inputs are finite; a program needn't handle non-finite values.
Results may differ from a plain program's by a relative error of at most 0.0055.
Values may be sent and summed in bfloat16 or wider, within the bound.
A program may use at most 64 MiB of HBM per device.

v0:
```python
import jax
import jax.numpy as jnp
from jax import lax
from jax.sharding import PartitionSpec as P

FIRST_DILATION = 4
SECOND_DILATION = 8


def padded(array, sides, width):
    for axis, dim in sides:
        peers, length = (lax.axis_size(axis), array.shape[dim])
        up = [(i, (i + 1) % peers) for i in range(peers - 1)]
        down = [(j, i) for i, j in up]
        last = lax.slice_in_dim(array, length - width, length, axis=dim)
        leading = lax.slice_in_dim(array, 0, width, axis=dim)
        before = lax.ppermute(last, axis, up)
        after = lax.ppermute(leading, axis, down)
        array = jnp.concatenate([before, array, after], axis=dim)
    return array


def swapped(value, axis, bit):
    mask = 2**bit
    pairs = [(source, source ^ mask) for source in range(lax.axis_size(axis))]
    return lax.ppermute(value, axis, pairs)


def dilated_conv(active, weight, spacing, out_rows, out_cols):
    windows = []
    for tap_row in range(3):
        for tap_col in range(3):
            windows.append(
                active[
                    tap_row * spacing : tap_row * spacing + out_rows,
                    tap_col * spacing : tap_col * spacing + out_cols,
                ]
            )
    stacked = jnp.concatenate(windows, axis=-1)
    flat_weight = weight.reshape(9 * weight.shape[2], weight.shape[3])
    return jnp.einsum("rch,hk->rck", stacked, flat_weight, preferred_element_type=jnp.float32)


def on_device(
    map_in,
    embedding,
    w_row,
    w_col,
    first_kernel_weight,
    first_bias,
    second_kernel_weight,
    second_bias,
    w_mix,
    b_mix,
    w_head,
):
    patch_rows, patch_columns, channels = map_in.shape
    row_count = lax.axis_size("row")
    row_at = lax.axis_index("row")
    col_at = lax.axis_index("col")
    all_bins = lax.all_gather(embedding, "row", axis=0, tiled=True)
    row_terms = jnp.dot(all_bins, w_row, preferred_element_type=jnp.float32)
    col_terms = jnp.dot(all_bins, w_col, preferred_element_type=jnp.float32)
    own_rows = lax.dynamic_slice_in_dim(row_terms, row_at * patch_rows, patch_rows, 0)
    own_cols = lax.dynamic_slice_in_dim(col_terms, col_at * patch_columns, patch_columns, 0)
    contact_grid = (
        map_in.astype(jnp.float32) + own_rows[:, None, :] + own_cols[None, :, :]
    ).astype(jnp.bfloat16)
    first_padded = padded(contact_grid, (("row", 0), ("col", 1)), FIRST_DILATION)
    first_layer = (
        contact_grid.astype(jnp.float32)
        + dilated_conv(
            jnp.maximum(first_padded, 0),
            first_kernel_weight,
            FIRST_DILATION,
            patch_rows,
            patch_columns,
        )
        + first_bias
    ).astype(jnp.bfloat16)
    second_padded = padded(first_layer, (("row", 0), ("col", 1)), SECOND_DILATION)
    second_layer = (
        first_layer.astype(jnp.float32)
        + dilated_conv(
            jnp.maximum(second_padded, 0),
            second_kernel_weight,
            SECOND_DILATION,
            patch_rows,
            patch_columns,
        )
        + second_bias
    ).astype(jnp.bfloat16)
    half_rows = patch_rows // 2
    blocks_per = row_count // 2
    arranged = second_layer.reshape(2, half_rows, blocks_per, patch_rows, channels)
    arranged = arranged.transpose(0, 2, 1, 3, 4).reshape(
        2 * blocks_per, half_rows, patch_rows, channels
    )
    exchanged = lax.all_to_all(
        lax.all_to_all(arranged, "row", split_axis=0, concat_axis=0, tiled=True),
        "col",
        split_axis=0,
        concat_axis=0,
        tiled=True,
    )
    exchanged = exchanged.reshape(2, blocks_per, half_rows, patch_rows, channels)
    top_half = row_at // blocks_per
    kept_part = lax.dynamic_index_in_dim(exchanged, top_half, 0, keepdims=False)
    sent_part = lax.dynamic_index_in_dim(exchanged, 1 - top_half, 0, keepdims=False)
    came_back = swapped(sent_part, "row", blocks_per.bit_length() - 1)
    stacked = jnp.where(
        top_half == 0, jnp.stack([kept_part, came_back]), jnp.stack([came_back, kept_part])
    )
    mirrored = stacked.transpose(3, 1, 0, 2, 4).reshape(patch_rows, patch_columns, channels)
    symmetric = ((second_layer.astype(jnp.float32) + mirrored.astype(jnp.float32)) * 0.5).astype(
        jnp.bfloat16
    )
    mixture = (
        jnp.einsum("rch,hk->rck", symmetric, w_mix, preferred_element_type=jnp.float32) + b_mix
    )
    mixture = jnp.maximum(mixture, 0.0)
    return jnp.sum(mixture * w_head, axis=-1)


def solution(mesh):
    placed = (
        P(("group", "row"), "col", None),
        P(("group", "row"), None),
        P(),
        P(),
        P(),
        P(),
        P(),
        P(),
        P(),
        P(),
        P(),
    )
    return jax.shard_map(
        on_device, mesh=mesh, in_specs=placed, out_specs=P(("group", "row"), "col"), check_vma=False
    )
```

profile of v0, /device:TPU:0, one launch (start us, length us, event | category | flops | bytes accessed | tf_op | source)
XLA Modules:
  0.0 92.6 jit_solution(15328792908924847365)
XLA Ops:
  0.0 0.7 copy-done.5
  0.7 32.3 %all-gather = bf16[8,12,96]{2,1,0:T(8,128)(2,1)S(1)} all-gather(bf16[1,12,96]{2,1,0:T(8,128)(2,1)S(1)} %bitcast.32), channel_id=1, replica_groups=mesh['group'=2,'row'=8,'col'=2] {'row'}, dimensions={0}, use_global_device_ids=true | all-gather | bytes 20736 | tf_op jit(solution)/shard_map/all_gather | solution.py:61
  34.0 3.4 %collective-permute-start = (bf16[4,48,48]{2,1,0:T(8,128)(2,1)S(1)}, bf16[4,48,48]{2,1,0:T(8,128)(2,1)S(1)}, u32[]{:S(2)}, u32[]{:S(2)}) collective-permute-start(bf16[4,48,48]{2,1,0:T(8,128)(2,1)S(1)} %get-tuple-element.31), channel_id=1, source_target_pairs={{0,2},{2,4},{4,6},{6,8},{8,10},{10,12},{12,14},{1,3},{3,5},{5,7},{... | collective-permute-start | bytes 55304 | tf_op jit(solution)/shard_map/ppermute | solution.py:17
  37.4 1.3 %collective-permute-start.1 = (bf16[4,48,48]{2,1,0:T(8,128)(2,1)S(1)}, bf16[4,48,48]{2,1,0:T(8,128)(2,1)S(1)}, u32[]{:S(2)}, u32[]{:S(2)}) collective-permute-start(bf16[4,48,48]{2,1,0:T(8,128)(2,1)S(1)} %get-tuple-element.32), channel_id=1, source_target_pairs={{2,0},{4,2},{6,4},{8,6},{10,8},{12,10},{14,12},{3,1},{5,3},{7,5},{... | collective-permute-start | bytes 55304 | tf_op jit(solution)/shard_map/ppermute | solution.py:18
  39.2 4.3 %collective-permute-done.1 = bf16[4,48,48]{2,1,0:T(8,128)(2,1)S(1)} collective-permute-done((bf16[4,48,48]{2,1,0:T(8,128)(2,1)S(1)}, bf16[4,48,48]{2,1,0:T(8,128)(2,1)S(1)}, u32[]{:S(2)}, u32[]{:S(2)}) %collective-permute-start.1) | collective-permute-done | bytes 18464 | tf_op jit(solution)/shard_map/ppermute | solution.py:18
  43.4 1.3 %collective-permute-start.2 = (bf16[20,4,48]{2,1,0:T(4,128)(2,1)S(1)}, bf16[20,4,48]{2,1,0:T(4,128)(2,1)S(1)}, u32[]{:S(2)}, u32[]{:S(2)}) collective-permute-start(bf16[20,4,48]{2,1,0:T(4,128)(2,1)S(1)} %get-tuple-element.25), channel_id=1, source_target_pairs={{0,1},{2,3},{4,5},{6,7},{8,9},{10,11},{12,13},{14,15},{16,17},{18,... | collective-permute-start | bytes 23048 | tf_op jit(solution)/shard_map/ppermute | solution.py:17
  44.7 1.3 %collective-permute-start.3 = (bf16[20,4,48]{2,1,0:T(4,128)(2,1)S(1)}, bf16[20,4,48]{2,1,0:T(4,128)(2,1)S(1)}, u32[]{:S(2)}, u32[]{:S(2)}) collective-permute-start(bf16[20,4,48]{2,1,0:T(4,128)(2,1)S(1)} %get-tuple-element.26), channel_id=1, source_target_pairs={{1,0},{3,2},{5,4},{7,6},{9,8},{11,10},{13,12},{15,14},{17,16},{19,... | collective-permute-start | bytes 23048 | tf_op jit(solution)/shard_map/ppermute | solution.py:18
  46.0 1.8 %collective-permute-done.3 = bf16[20,4,48]{2,1,0:T(4,128)(2,1)S(1)} collective-permute-done((bf16[20,4,48]{2,1,0:T(4,128)(2,1)S(1)}, bf16[20,4,48]{2,1,0:T(4,128)(2,1)S(1)}, u32[]{:S(2)}, u32[]{:S(2)}) %collective-permute-start.3) | collective-permute-done | bytes 7712 | tf_op jit(solution)/shard_map/ppermute | solution.py:18
  48.2 0.6 concatenate.20
  48.8 0.6 copy-done.6
  49.8 2.8 %collective-permute-start.4 = (bf16[8,48,48]{2,1,0:T(8,128)(2,1)S(1)}, bf16[8,48,48]{2,1,0:T(8,128)(2,1)S(1)}, u32[]{:S(2)}, u32[]{:S(2)}) collective-permute-start(bf16[8,48,48]{2,1,0:T(8,128)(2,1)S(1)} %get-tuple-element.29), channel_id=1, source_target_pairs={{0,2},{2,4},{4,6},{6,8},{8,10},{10,12},{12,14},{1,3},{3,5},{5,7},{... | collective-permute-start | bytes 110600 | tf_op jit(solution)/shard_map/ppermute | solution.py:17
  52.7 1.3 %collective-permute-start.5 = (bf16[8,48,48]{2,1,0:T(8,128)(2,1)S(1)}, bf16[8,48,48]{2,1,0:T(8,128)(2,1)S(1)}, u32[]{:S(2)}, u32[]{:S(2)}) collective-permute-start(bf16[8,48,48]{2,1,0:T(8,128)(2,1)S(1)} %get-tuple-element.30), channel_id=1, source_target_pairs={{2,0},{4,2},{6,4},{8,6},{10,8},{12,10},{14,12},{3,1},{5,3},{7,5},{... | collective-permute-start | bytes 110600 | tf_op jit(solution)/shard_map/ppermute | solution.py:18
  54.0 1.1 %collective-permute-done.4 = bf16[8,48,48]{2,1,0:T(8,128)(2,1)S(1)} collective-permute-done((bf16[8,48,48]{2,1,0:T(8,128)(2,1)S(1)}, bf16[8,48,48]{2,1,0:T(8,128)(2,1)S(1)}, u32[]{:S(2)}, u32[]{:S(2)}) %collective-permute-start.4) | collective-permute-done | bytes 36896 | tf_op jit(solution)/shard_map/ppermute | solution.py:17
  55.0 4.2 %collective-permute-done.5 = bf16[8,48,48]{2,1,0:T(8,128)(2,1)S(1)} collective-permute-done((bf16[8,48,48]{2,1,0:T(8,128)(2,1)S(1)}, bf16[8,48,48]{2,1,0:T(8,128)(2,1)S(1)}, u32[]{:S(2)}, u32[]{:S(2)}) %collective-permute-start.5) | collective-permute-done | bytes 36896 | tf_op jit(solution)/shard_map/ppermute | solution.py:18
  59.2 1.3 %collective-permute-start.6 = (bf16[28,8,48]{2,1,0:T(8,128)(2,1)S(1)}, bf16[28,8,48]{2,1,0:T(8,128)(2,1)S(1)}, u32[]{:S(2)}, u32[]{:S(2)}) collective-permute-start(bf16[28,8,48]{2,1,0:T(8,128)(2,1)S(1)} %get-tuple-element.14), channel_id=1, source_target_pairs={{0,1},{2,3},{4,5},{6,7},{8,9},{10,11},{12,13},{14,15},{16,17},{18,... | collective-permute-start | bytes 64520 | tf_op jit(solution)/shard_map/ppermute | solution.py:17
  60.5 1.3 %collective-permute-start.7 = (bf16[28,8,48]{2,1,0:T(8,128)(2,1)S(1)}, bf16[28,8,48]{2,1,0:T(8,128)(2,1)S(1)}, u32[]{:S(2)}, u32[]{:S(2)}) collective-permute-start(bf16[28,8,48]{2,1,0:T(8,128)(2,1)S(1)} %get-tuple-element.15), channel_id=1, source_target_pairs={{1,0},{3,2},{5,4},{7,6},{9,8},{11,10},{13,12},{15,14},{17,16},{19,... | collective-permute-start | bytes 64520 | tf_op jit(solution)/shard_map/ppermute | solution.py:18
  61.8 1.8 %collective-permute-done.7 = bf16[28,8,48]{2,1,0:T(8,128)(2,1)S(1)} collective-permute-done((bf16[28,8,48]{2,1,0:T(8,128)(2,1)S(1)}, bf16[28,8,48]{2,1,0:T(8,128)(2,1)S(1)}, u32[]{:S(2)}, u32[]{:S(2)}) %collective-permute-start.7) | collective-permute-done | bytes 21536 | tf_op jit(solution)/shard_map/ppermute | solution.py:18
  64.0 0.6 concatenate.23
  65.8 0.8 reshape.35
  66.6 6.0 %all-to-all-start = ((bf16[8,2,1728]{2,1,0:T(2,128)(2,1)}), bf16[8,2,1728]{2,1,0:T(2,128)(2,1)S(1)}, u32[]{:S(2)}, u32[]{:S(2)}) async-start(bf16[8,2,1728]{2,1,0:T(2,128)(2,1)} %reshape.35), calls=%async_computation | async-start | bytes 114688 | tf_op jit(solution)/shard_map/all_to_all | solution.py:100
  72.6 6.8 %all-to-all-done = bf16[8,2,1728]{2,1,0:T(2,128)(2,1)S(1)} async-done(((bf16[8,2,1728]{2,1,0:T(2,128)(2,1)}), bf16[8,2,1728]{2,1,0:T(2,128)(2,1)S(1)}, u32[]{:S(2)}, u32[]{:S(2)}) %all-to-all-start) | async-done | bytes 55328 | tf_op jit(solution)/shard_map/all_to_all | solution.py:100
  79.9 3.8 %all_to_all.10 = bf16[2,2,6912]{2,1,0:T(2,128)(2,1)S(1)} all-to-all(bf16[2,2,6912]{2,1,0:T(2,128)(2,1)S(1)} %reshape.37), channel_id=1, replica_groups=mesh['group'=2,'row'=8,'col'=2] {'col'}, dimensions={0} | all-to-all | bytes 110592 | tf_op jit(solution)/shard_map/all_to_all | solution.py:99
  84.6 6.0 %collective-permute-done.8 = bf16[4,6,12,48]{3,0,2,1:T(4,128)(2,1)S(1)} collective-permute-done((bf16[4,6,12,48]{3,0,2,1:T(4,128)(2,1)S(1)}, bf16[4,6,12,48]{3,0,2,1:T(4,128)(2,1)S(1)}, u32[]{:S(2)}, u32[]{:S(2)}) %collective-permute-start.8) | collective-permute-done | bytes 27680 | tf_op jit(solution)/shard_map/ppermute | solution.py:26
  91.7 0.9 fusion.6
  (51 shorter events, 5.9 us)
Async XLA Ops:
  0.0 48.8 %copy-start = (bf16[3,3,48,48]{3,2,1,0:T(8,128)(2,1)S(1)}, bf16[3,3,48,48]{3,2,1,0:T(8,128)(2,1)}, u32[]{:S(2)}) copy-start(bf16[3,3,48,48]{3,2,1,0:T(8,128)(2,1)} %param.15) | copy-start | bytes 124420
  0.0 0.7 copy-start.5
  0.7 32.3 %copy-start.3 = (bf16[96,48]{0,1:T(8,128)(2,1)S(1)}, bf16[96,48]{0,1:T(8,128)(2,1)}, u32[]{:S(2)}) copy-start(bf16[96,48]{0,1:T(8,128)(2,1)} %param.13) | copy-start | bytes 27652
  0.7 32.5 %copy-start.4 = (bf16[96,48]{0,1:T(8,128)(2,1)S(1)}, bf16[96,48]{0,1:T(8,128)(2,1)}, u32[]{:S(2)}) copy-start(bf16[96,48]{0,1:T(8,128)(2,1)} %param.14) | copy-start | bytes 27652
  33.0 0.9 copy-start.1
  34.0 5.1 %collective-permute-start = (bf16[4,48,48]{2,1,0:T(8,128)(2,1)S(1)}, bf16[4,48,48]{2,1,0:T(8,128)(2,1)S(1)}, u32[]{:S(2)}, u32[]{:S(2)}) collective-permute-start(bf16[4,48,48]{2,1,0:T(8,128)(2,1)S(1)} %get-tuple-element.31), channel_id=1, source_target_pairs={{0,2},{2,4},{4,6},{6,8},{8,10},{10,12},{12,14},{1,3},{3,5},{5,7},{... | collective-permute-start | bytes 55304 | tf_op jit(solution)/shard_map/ppermute | solution.py:17
  37.4 6.0 %collective-permute-start.1 = (bf16[4,48,48]{2,1,0:T(8,128)(2,1)S(1)}, bf16[4,48,48]{2,1,0:T(8,128)(2,1)S(1)}, u32[]{:S(2)}, u32[]{:S(2)}) collective-permute-start(bf16[4,48,48]{2,1,0:T(8,128)(2,1)S(1)} %get-tuple-element.32), channel_id=1, source_target_pairs={{2,0},{4,2},{6,4},{8,6},{10,8},{12,10},{14,12},{3,1},{5,3},{7,5},{... | collective-permute-start | bytes 55304 | tf_op jit(solution)/shard_map/ppermute | solution.py:18
  43.4 2.6 %collective-permute-start.2 = (bf16[20,4,48]{2,1,0:T(4,128)(2,1)S(1)}, bf16[20,4,48]{2,1,0:T(4,128)(2,1)S(1)}, u32[]{:S(2)}, u32[]{:S(2)}) collective-permute-start(bf16[20,4,48]{2,1,0:T(4,128)(2,1)S(1)} %get-tuple-element.25), channel_id=1, source_target_pairs={{0,1},{2,3},{4,5},{6,7},{8,9},{10,11},{12,13},{14,15},{16,17},{18,... | collective-permute-start | bytes 23048 | tf_op jit(solution)/shard_map/ppermute | solution.py:17
  44.7 3.1 %collective-permute-start.3 = (bf16[20,4,48]{2,1,0:T(4,128)(2,1)S(1)}, bf16[20,4,48]{2,1,0:T(4,128)(2,1)S(1)}, u32[]{:S(2)}, u32[]{:S(2)}) collective-permute-start(bf16[20,4,48]{2,1,0:T(4,128)(2,1)S(1)} %get-tuple-element.26), channel_id=1, source_target_pairs={{1,0},{3,2},{5,4},{7,6},{9,8},{11,10},{13,12},{15,14},{17,16},{19,... | collective-permute-start | bytes 23048 | tf_op jit(solution)/shard_map/ppermute | solution.py:18
  48.8 0.7 copy-start.6
  49.8 5.2 %collective-permute-start.4 = (bf16[8,48,48]{2,1,0:T(8,128)(2,1)S(1)}, bf16[8,48,48]{2,1,0:T(8,128)(2,1)S(1)}, u32[]{:S(2)}, u32[]{:S(2)}) collective-permute-start(bf16[8,48,48]{2,1,0:T(8,128)(2,1)S(1)} %get-tuple-element.29), channel_id=1, source_target_pairs={{0,2},{2,4},{4,6},{6,8},{8,10},{10,12},{12,14},{1,3},{3,5},{5,7},{... | collective-permute-start | bytes 110600 | tf_op jit(solution)/shard_map/ppermute | solution.py:17
  52.7 6.5 %collective-permute-start.5 = (bf16[8,48,48]{2,1,0:T(8,128)(2,1)S(1)}, bf16[8,48,48]{2,1,0:T(8,128)(2,1)S(1)}, u32[]{:S(2)}, u32[]{:S(2)}) collective-permute-start(bf16[8,48,48]{2,1,0:T(8,128)(2,1)S(1)} %get-tuple-element.30), channel_id=1, source_target_pairs={{2,0},{4,2},{6,4},{8,6},{10,8},{12,10},{14,12},{3,1},{5,3},{7,5},{... | collective-permute-start | bytes 110600 | tf_op jit(solution)/shard_map/ppermute | solution.py:18
  59.2 2.6 %collective-permute-start.6 = (bf16[28,8,48]{2,1,0:T(8,128)(2,1)S(1)}, bf16[28,8,48]{2,1,0:T(8,128)(2,1)S(1)}, u32[]{:S(2)}, u32[]{:S(2)}) collective-permute-start(bf16[28,8,48]{2,1,0:T(8,128)(2,1)S(1)} %get-tuple-element.14), channel_id=1, source_target_pairs={{0,1},{2,3},{4,5},{6,7},{8,9},{10,11},{12,13},{14,15},{16,17},{18,... | collective-permute-start | bytes 64520 | tf_op jit(solution)/shard_map/ppermute | solution.py:17
  60.5 3.1 %collective-permute-start.7 = (bf16[28,8,48]{2,1,0:T(8,128)(2,1)S(1)}, bf16[28,8,48]{2,1,0:T(8,128)(2,1)S(1)}, u32[]{:S(2)}, u32[]{:S(2)}) collective-permute-start(bf16[28,8,48]{2,1,0:T(8,128)(2,1)S(1)} %get-tuple-element.15), channel_id=1, source_target_pairs={{1,0},{3,2},{5,4},{7,6},{9,8},{11,10},{13,12},{15,14},{17,16},{19,... | collective-permute-start | bytes 64520 | tf_op jit(solution)/shard_map/ppermute | solution.py:18
  64.0 0.9 copy-start.2
  64.6 0.7 copy-start.7
  66.6 12.8 %all-to-all-start = ((bf16[8,2,1728]{2,1,0:T(2,128)(2,1)}), bf16[8,2,1728]{2,1,0:T(2,128)(2,1)S(1)}, u32[]{:S(2)}, u32[]{:S(2)}) async-start(bf16[8,2,1728]{2,1,0:T(2,128)(2,1)} %reshape.35), calls=%async_computation | async-start | bytes 114688 | tf_op jit(solution)/shard_map/all_to_all | solution.py:100
  84.1 6.6 %collective-permute-start.8 = (bf16[4,6,12,48]{3,0,2,1:T(4,128)(2,1)S(1)}, bf16[4,6,12,48]{3,0,2,1:T(4,128)(2,1)S(1)}, u32[]{:S(2)}, u32[]{:S(2)}) collective-permute-start(bf16[4,6,12,48]{3,0,2,1:T(4,128)(2,1)S(1)} %get-tuple-element.28), channel_id=1, source_target_pairs={{0,8},{2,10},{4,12},{6,14},{8,0},{10,2},{12,4},{14,6},{1,9},{3,11}... | collective-permute-start | bytes 82952 | tf_op jit(solution)/shard_map/ppermute | solution.py:26
  91.0 0.7 copy-start.8
  91.0 0.7 copy-start.9
  91.0 0.7 copy-start.10
where the time goes:
time: 93.2 us; the launch traced here: 92.6 us
  blocking collectives  36.1 us (39%)
  waiting for transfers between devices  26.4 us (28%)
  starting transfers between devices  20.5 us (22%)
  local copies, waits for them, and re-layouts  7.02 us (8%)
  matrix products  1.8 us (2%)
    all_gather x1, blocking collectives, on_device(): all_bins = lax.all_gather(embedding, 'row', axis=0, tiled=True)  32.3 us
    ppermute x4, waiting for transfers between devices, padded(): after = lax.ppermute(leading, axis, down)  12 us
    ppermute x4, starting transfers between devices, padded(): before = lax.ppermute(last, axis, up)  8.8 us
    all_to_all x1, waiting for transfers between devices, on_device(): lax.all_to_all(arranged, 'row', split_axis=0, concat_axis=0, tiled=True)  6.85 us
    ppermute x1, waiting for transfers between devices, swapped(): return lax.ppermute(value, axis, pairs)  6.02 us
    all_to_all x1, starting transfers between devices, on_device(): lax.all_to_all(arranged, 'row', split_axis=0, concat_axis=0, tiled=True)  5.98 us
    ppermute x4, starting transfers between devices, padded(): after = lax.ppermute(leading, axis, down)  5.17 us
    unnamed x27, local copies, waits for them, and re-layouts  4.82 us
  transfers between devices with their start and end apart: 10, of which 8 were waited for; matrix products, arithmetic and copies ran while one was open for 0% of the time, Pallas kernels for 0%

commit v1 on v0

--- a/solution.py
+++ b/solution.py
@@ -2,6 +2,7 @@
 import jax.numpy as jnp
 from jax import lax
 from jax.sharding import PartitionSpec as P
+from jax.lax import axis_index, ppermute, psum
 
 FIRST_DILATION = 4
 SECOND_DILATION = 8
@@ -58,7 +59,22 @@
     row_count = lax.axis_size("row")
     row_at = lax.axis_index("row")
     col_at = lax.axis_index("col")
-    all_bins = lax.all_gather(embedding, "row", axis=0, tiled=True)
+    field_out, seen_now, out_arr = (psum(1, axis_name="row"), axis_index("row"), embedding.shape[0])
+    prior, row_out = (embedding, 1)
+    while row_out < field_out:
+        prior = jnp.concatenate(
+            [
+                prior,
+                ppermute(
+                    prior,
+                    axis_name="row",
+                    perm=tuple(((jj, (jj - row_out) % field_out) for jj in range(field_out))),
+                ),
+            ],
+            axis=0,
+        )
+        row_out = 2 * row_out
+    all_bins = jnp.roll(prior, seen_now * out_arr, axis=0)
     row_terms = jnp.dot(all_bins, w_row, preferred_element_type=jnp.float32)
     col_terms = jnp.dot(all_bins, w_col, preferred_element_type=jnp.float32)
     own_rows = lax.dynamic_slice_in_dim(row_terms, row_at * patch_rows, patch_rows, 0)

time: 93.2 us -> 80.3 us (0.86)
  blocking collectives: 36.1 us -> 3.77 us
  starting transfers between devices: 20.5 us -> 32.3 us
  waiting for transfers between devices: 26.4 us -> 33.7 us
    all_gather x1 -> x0, blocking collectives: 32.3 us -> none  [on_device(): all_bins = lax.all_gather(embedding, 'row', axis=0, tiled=True)]
    ppermute x0 -> x3, waiting for transfers between devices: none -> 8.07 us  [on_device(): ppermute(prior, axis_name='row', perm=tuple(((jj, (jj - row_out) % field_...]
    ppermute x0 -> x3, starting transfers between devices: none -> 7.73 us  [on_device(): ppermute(prior, axis_name='row', perm=tuple(((jj, (jj - row_out) % field_...]
    ppermute x4, starting transfers between devices: 8.8 us -> 12.6 us  [padded(): before = lax.ppermute(last, axis, up)]
    ppermute x4, waiting for transfers between devices: 12 us -> 10.4 us  [padded(): after = lax.ppermute(leading, axis, down)]
    unnamed x27 -> x26, local copies, waits for them, and re-layouts: 4.82 us -> 4.08 us
  transfers between devices with their start and end apart: 10 -> 13, of which waited for: 8 -> 11; matrix products, arithmetic and copies ran while one was open for 0% -> 0% of each run, Pallas kernels for 0% -> 0%
where the time goes in v1:
time: 80.3 us; the launch traced here: 79.7 us
  waiting for transfers between devices  33.7 us (42%)
  starting transfers between devices  32.3 us (40%)
  local copies, waits for them, and re-layouts  6.49 us (8%)
  blocking collectives  3.77 us (5%)
  matrix products  1.81 us (2%)
  other arithmetic  1.23 us (2%)
    ppermute x4, starting transfers between devices, padded(): before = lax.ppermute(last, axis, up)  12.6 us
    ppermute x4, waiting for transfers between devices, padded(): after = lax.ppermute(leading, axis, down)  10.4 us
    ppermute x3, waiting for transfers between devices, on_device(): ppermute(prior, axis_name='row', perm=tuple(((jj, (jj - row_out) % field_...  8.07 us
    ppermute x3, starting transfers between devices, on_device(): ppermute(prior, axis_name='row', perm=tuple(((jj, (jj - row_out) % field_...  7.73 us
    all_to_all x1, waiting for transfers between devices, on_device(): lax.all_to_all(arranged, 'row', split_axis=0, concat_axis=0, tiled=True)  6.85 us
    all_to_all x1, starting transfers between devices, on_device(): lax.all_to_all(arranged, 'row', split_axis=0, concat_axis=0, tiled=True)  6.29 us
    ppermute x1, waiting for transfers between devices, swapped(): return lax.ppermute(value, axis, pairs)  6.02 us
    ppermute x4, starting transfers between devices, padded(): after = lax.ppermute(leading, axis, down)  5.17 us
  transfers between devices with their start and end apart: 13, of which 11 were waited for; matrix products, arithmetic and copies ran while one was open for 0% of the time, Pallas kernels for 0%

profile of v1, /device:TPU:0, one launch (start us, length us, event | category | flops | bytes accessed | tf_op | source)
XLA Modules:
  0.0 79.7 jit_solution(3860093857542430630)
XLA Ops:
  0.0 6.0 %collective-permute-start = (bf16[12,96]{1,0:T(8,128)(2,1)}, bf16[12,96]{1,0:T(8,128)(2,1)S(1)}, u32[]{:S(2)}, u32[]{:S(2)}) collective-permute-start(bf16[12,96]{1,0:T(8,128)(2,1)} %param.12), channel_id=1, source_target_pairs={{0,14},{2,0},{4,2},{6,4},{8,6},{10,8},{12,10},{14,12},{1,15},{3,1}... | collective-permute-start | bytes 6920 | tf_op jit(solution)/shard_map/ppermute | solution.py:68
  6.0 1.5 %collective-permute-done = bf16[12,96]{1,0:T(8,128)(2,1)S(1)} collective-permute-done((bf16[12,96]{1,0:T(8,128)(2,1)}, bf16[12,96]{1,0:T(8,128)(2,1)S(1)}, u32[]{:S(2)}, u32[]{:S(2)}) %collective-permute-start) | collective-permute-done | bytes 2336 | tf_op jit(solution)/shard_map/ppermute | solution.py:68
  8.2 1.4 %collective-permute-start.1 = (bf16[24,96]{1,0:T(8,128)(2,1)S(1)}, bf16[24,96]{1,0:T(8,128)(2,1)S(1)}, u32[]{:S(2)}, u32[]{:S(2)}) collective-permute-start(bf16[24,96]{1,0:T(8,128)(2,1)S(1)} %pad_maximum_fusion.7), channel_id=1, source_target_pairs={{0,12},{2,14},{4,0},{6,2},{8,4},{10,6},{12,8},{14,10},{1,13},{3,15... | collective-permute-start | bytes 13832 | tf_op jit(solution)/shard_map/ppermute | solution.py:68
  9.6 2.3 %collective-permute-done.1 = bf16[24,96]{1,0:T(8,128)(2,1)S(1)} collective-permute-done((bf16[24,96]{1,0:T(8,128)(2,1)S(1)}, bf16[24,96]{1,0:T(8,128)(2,1)S(1)}, u32[]{:S(2)}, u32[]{:S(2)}) %collective-permute-start.1) | collective-permute-done | bytes 4640 | tf_op jit(solution)/shard_map/ppermute | solution.py:68
  12.3 4.3 %collective-permute-done.2 = bf16[48,96]{1,0:T(8,128)(2,1)S(1)} collective-permute-done((bf16[48,96]{1,0:T(8,128)(2,1)S(1)}, bf16[48,96]{1,0:T(8,128)(2,1)S(1)}, u32[]{:S(2)}, u32[]{:S(2)}) %collective-permute-start.2) | collective-permute-done | bytes 9248 | tf_op jit(solution)/shard_map/ppermute | solution.py:68
  17.7 5.2 %collective-permute-start.3 = (bf16[4,48,48]{2,1,0:T(8,128)(2,1)S(1)}, bf16[4,48,48]{2,1,0:T(8,128)(2,1)S(1)}, u32[]{:S(2)}, u32[]{:S(2)}) collective-permute-start(bf16[4,48,48]{2,1,0:T(8,128)(2,1)S(1)} %get-tuple-element.31), channel_id=1, source_target_pairs={{0,2},{2,4},{4,6},{6,8},{8,10},{10,12},{12,14},{1,3},{3,5},{5,7},{... | collective-permute-start | bytes 55304 | tf_op jit(solution)/shard_map/ppermute | solution.py:18
  22.9 1.3 %collective-permute-start.4 = (bf16[4,48,48]{2,1,0:T(8,128)(2,1)S(1)}, bf16[4,48,48]{2,1,0:T(8,128)(2,1)S(1)}, u32[]{:S(2)}, u32[]{:S(2)}) collective-permute-start(bf16[4,48,48]{2,1,0:T(8,128)(2,1)S(1)} %get-tuple-element.32), channel_id=1, source_target_pairs={{2,0},{4,2},{6,4},{8,6},{10,8},{12,10},{14,12},{3,1},{5,3},{7,5},{... | collective-permute-start | bytes 55304 | tf_op jit(solution)/shard_map/ppermute | solution.py:19
  24.6 4.3 %collective-permute-done.4 = bf16[4,48,48]{2,1,0:T(8,128)(2,1)S(1)} collective-permute-done((bf16[4,48,48]{2,1,0:T(8,128)(2,1)S(1)}, bf16[4,48,48]{2,1,0:T(8,128)(2,1)S(1)}, u32[]{:S(2)}, u32[]{:S(2)}) %collective-permute-start.4) | collective-permute-done | bytes 18464 | tf_op jit(solution)/shard_map/ppermute | solution.py:19
  28.9 1.3 %collective-permute-start.5 = (bf16[20,4,48]{2,1,0:T(4,128)(2,1)S(1)}, bf16[20,4,48]{2,1,0:T(4,128)(2,1)S(1)}, u32[]{:S(2)}, u32[]{:S(2)}) collective-permute-start(bf16[20,4,48]{2,1,0:T(4,128)(2,1)S(1)} %get-tuple-element.25), channel_id=1, source_target_pairs={{0,1},{2,3},{4,5},{6,7},{8,9},{10,11},{12,13},{14,15},{16,17},{18,... | collective-permute-start | bytes 23048 | tf_op jit(solution)/shard_map/ppermute | solution.py:18
  30.2 1.3 %collective-permute-start.6 = (bf16[20,4,48]{2,1,0:T(4,128)(2,1)S(1)}, bf16[20,4,48]{2,1,0:T(4,128)(2,1)S(1)}, u32[]{:S(2)}, u32[]{:S(2)}) collective-permute-start(bf16[20,4,48]{2,1,0:T(4,128)(2,1)S(1)} %get-tuple-element.26), channel_id=1, source_target_pairs={{1,0},{3,2},{5,4},{7,6},{9,8},{11,10},{13,12},{15,14},{17,16},{19,... | collective-permute-start | bytes 23048 | tf_op jit(solution)/shard_map/ppermute | solution.py:19
  31.5 1.8 %collective-permute-done.6 = bf16[20,4,48]{2,1,0:T(4,128)(2,1)S(1)} collective-permute-done((bf16[20,4,48]{2,1,0:T(4,128)(2,1)S(1)}, bf16[20,4,48]{2,1,0:T(4,128)(2,1)S(1)}, u32[]{:S(2)}, u32[]{:S(2)}) %collective-permute-start.6) | collective-permute-done | bytes 7712 | tf_op jit(solution)/shard_map/ppermute | solution.py:19
  35.3 3.1 %collective-permute-start.7 = (bf16[8,48,48]{2,1,0:T(8,128)(2,1)S(1)}, bf16[8,48,48]{2,1,0:T(8,128)(2,1)S(1)}, u32[]{:S(2)}, u32[]{:S(2)}) collective-permute-start(bf16[8,48,48]{2,1,0:T(8,128)(2,1)S(1)} %get-tuple-element.29), channel_id=1, source_target_pairs={{0,2},{2,4},{4,6},{6,8},{8,10},{10,12},{12,14},{1,3},{3,5},{5,7},{... | collective-permute-start | bytes 110600 | tf_op jit(solution)/shard_map/ppermute | solution.py:18
  38.4 1.3 %collective-permute-start.8 = (bf16[8,48,48]{2,1,0:T(8,128)(2,1)S(1)}, bf16[8,48,48]{2,1,0:T(8,128)(2,1)S(1)}, u32[]{:S(2)}, u32[]{:S(2)}) collective-permute-start(bf16[8,48,48]{2,1,0:T(8,128)(2,1)S(1)} %get-tuple-element.30), channel_id=1, source_target_pairs={{2,0},{4,2},{6,4},{8,6},{10,8},{12,10},{14,12},{3,1},{5,3},{7,5},{... | collective-permute-start | bytes 110600 | tf_op jit(solution)/shard_map/ppermute | solution.py:19
  39.7 1.1 %collective-permute-done.7 = bf16[8,48,48]{2,1,0:T(8,128)(2,1)S(1)} collective-permute-done((bf16[8,48,48]{2,1,0:T(8,128)(2,1)S(1)}, bf16[8,48,48]{2,1,0:T(8,128)(2,1)S(1)}, u32[]{:S(2)}, u32[]{:S(2)}) %collective-permute-start.7) | collective-permute-done | bytes 36896 | tf_op jit(solution)/shard_map/ppermute | solution.py:18
  40.7 4.4 %collective-permute-done.8 = bf16[8,48,48]{2,1,0:T(8,128)(2,1)S(1)} collective-permute-done((bf16[8,48,48]{2,1,0:T(8,128)(2,1)S(1)}, bf16[8,48,48]{2,1,0:T(8,128)(2,1)S(1)}, u32[]{:S(2)}, u32[]{:S(2)}) %collective-permute-start.8) | collective-permute-done | bytes 36896 | tf_op jit(solution)/shard_map/ppermute | solution.py:19
  45.1 1.3 %collective-permute-start.10 = (bf16[28,8,48]{2,1,0:T(8,128)(2,1)S(1)}, bf16[28,8,48]{2,1,0:T(8,128)(2,1)S(1)}, u32[]{:S(2)}, u32[]{:S(2)}) collective-permute-start(bf16[28,8,48]{2,1,0:T(8,128)(2,1)S(1)} %get-tuple-element.15), channel_id=1, source_target_pairs={{1,0},{3,2},{5,4},{7,6},{9,8},{11,10},{13,12},{15,14},{17,16},{19,... | collective-permute-start | bytes 64520 | tf_op jit(solution)/shard_map/ppermute | solution.py:19
  46.4 3.0 %collective-permute-start.9 = (bf16[28,8,48]{2,1,0:T(8,128)(2,1)S(1)}, bf16[28,8,48]{2,1,0:T(8,128)(2,1)S(1)}, u32[]{:S(2)}, u32[]{:S(2)}) collective-permute-start(bf16[28,8,48]{2,1,0:T(8,128)(2,1)S(1)} %get-tuple-element.14), channel_id=1, source_target_pairs={{0,1},{2,3},{4,5},{6,7},{8,9},{10,11},{12,13},{14,15},{16,17},{18,... | collective-permute-start | bytes 64520 | tf_op jit(solution)/shard_map/ppermute | solution.py:18
  49.5 0.9 %collective-permute-done.9 = bf16[28,8,48]{2,1,0:T(8,128)(2,1)S(1)} collective-permute-done((bf16[28,8,48]{2,1,0:T(8,128)(2,1)S(1)}, bf16[28,8,48]{2,1,0:T(8,128)(2,1)S(1)}, u32[]{:S(2)}, u32[]{:S(2)}) %collective-permute-start.9) | collective-permute-done | bytes 21536 | tf_op jit(solution)/shard_map/ppermute | solution.py:18
  52.5 0.8 %reshape.33 = bf16[8,2,1728]{2,1,0:T(2,128)(2,1)} reshape(bf16[8,6,12,48]{3,2,1,0:T(8,128)(2,1)S(1)} %copy.23) | data formatting | bytes 110592
  53.3 6.3 %all-to-all-start = ((bf16[8,2,1728]{2,1,0:T(2,128)(2,1)}), bf16[8,2,1728]{2,1,0:T(2,128)(2,1)S(1)}, u32[]{:S(2)}, u32[]{:S(2)}) async-start(bf16[8,2,1728]{2,1,0:T(2,128)(2,1)} %reshape.33), calls=%async_computation | async-start | bytes 114688 | tf_op jit(solution)/shard_map/all_to_all | solution.py:116
  59.6 6.8 %all-to-all-done = bf16[8,2,1728]{2,1,0:T(2,128)(2,1)S(1)} async-done(((bf16[8,2,1728]{2,1,0:T(2,128)(2,1)}), bf16[8,2,1728]{2,1,0:T(2,128)(2,1)S(1)}, u32[]{:S(2)}, u32[]{:S(2)}) %all-to-all-start) | async-done | bytes 55328 | tf_op jit(solution)/shard_map/all_to_all | solution.py:116
  66.9 3.8 %all_to_all.10 = bf16[2,2,6912]{2,1,0:T(2,128)(2,1)S(1)} all-to-all(bf16[2,2,6912]{2,1,0:T(2,128)(2,1)S(1)} %reshape.35), channel_id=1, replica_groups=mesh['group'=2,'row'=8,'col'=2] {'col'}, dimensions={0} | all-to-all | bytes 110592 | tf_op jit(solution)/shard_map/all_to_all | solution.py:115
  71.7 6.0 %collective-permute-done.11 = bf16[4,6,12,48]{3,0,2,1:T(4,128)(2,1)S(1)} collective-permute-done((bf16[4,6,12,48]{3,0,2,1:T(4,128)(2,1)S(1)}, bf16[4,6,12,48]{3,0,2,1:T(4,128)(2,1)S(1)}, u32[]{:S(2)}, u32[]{:S(2)}) %collective-permute-start.11) | collective-permute-done | bytes 27680 | tf_op jit(solution)/shard_map/ppermute | solution.py:27
  78.8 0.9 %fusion.6 = f32[12,48]{1,0:T(8,128)} fusion(f32[12,48,48]{2,1,0:T(8,128)S(1)} %reshape.29, bf16[12,48,48]{2,1,0:T(8,128)(2,1)S(1)} %fusion.4, f32[48]{0:T(128)S(1)} %copy-done.9, f32[48]{0:T(128)S(1)} %copy-done.10, bf16[48,48]{1,0:T(8,128)(2,1)S(1)} %copy-done.8), kind=kOutput, calls=%fused_computation.9 | convolution fusion | flops 2874816 | bytes 173184 | tf_op jit(solution)/shard_map/rch,hk->rck/dot_general | solution.py:135
  (58 shorter events, 9.2 us)
Async XLA Ops:
  0.0 34.3 %copy-start = (bf16[3,3,48,48]{3,2,1,0:T(8,128)(2,1)S(1)}, bf16[3,3,48,48]{3,2,1,0:T(8,128)(2,1)}, u32[]{:S(2)}) copy-start(bf16[3,3,48,48]{3,2,1,0:T(8,128)(2,1)} %param.15) | copy-start | bytes 124420
  0.0 11.8 %copy-start.3 = (bf16[12,96]{1,0:T(8,128)(2,1)S(1)}, bf16[12,96]{1,0:T(8,128)(2,1)}, u32[]{:S(2)}) copy-start(bf16[12,96]{1,0:T(8,128)(2,1)} %param.12) | copy-start | bytes 6916
  0.0 7.5 %collective-permute-start = (bf16[12,96]{1,0:T(8,128)(2,1)}, bf16[12,96]{1,0:T(8,128)(2,1)S(1)}, u32[]{:S(2)}, u32[]{:S(2)}) collective-permute-start(bf16[12,96]{1,0:T(8,128)(2,1)} %param.12), channel_id=1, source_target_pairs={{0,14},{2,0},{4,2},{6,4},{8,6},{10,8},{12,10},{14,12},{1,15},{3,1}... | collective-permute-start | bytes 6920 | tf_op jit(solution)/shard_map/ppermute | solution.py:68
  8.2 3.6 %collective-permute-start.1 = (bf16[24,96]{1,0:T(8,128)(2,1)S(1)}, bf16[24,96]{1,0:T(8,128)(2,1)S(1)}, u32[]{:S(2)}, u32[]{:S(2)}) collective-permute-start(bf16[24,96]{1,0:T(8,128)(2,1)S(1)} %pad_maximum_fusion.7), channel_id=1, source_target_pairs={{0,12},{2,14},{4,0},{6,2},{8,4},{10,6},{12,8},{14,10},{1,13},{3,15... | collective-permute-start | bytes 13832 | tf_op jit(solution)/shard_map/ppermute | solution.py:68
  11.9 4.7 %collective-permute-start.2 = (bf16[48,96]{1,0:T(8,128)(2,1)S(1)}, bf16[48,96]{1,0:T(8,128)(2,1)S(1)}, u32[]{:S(2)}, u32[]{:S(2)}) collective-permute-start(bf16[48,96]{1,0:T(8,128)(2,1)S(1)} %pad_maximum_fusion.6), channel_id=1, source_target_pairs={{0,8},{2,10},{4,12},{6,14},{8,0},{10,2},{12,4},{14,6},{1,9},{3,11}... | collective-permute-start | bytes 27656 | tf_op jit(solution)/shard_map/ppermute | solution.py:68
  12.3 4.5 %copy-start.4 = (bf16[96,48]{0,1:T(8,128)(2,1)S(1)}, bf16[96,48]{0,1:T(8,128)(2,1)}, u32[]{:S(2)}) copy-start(bf16[96,48]{0,1:T(8,128)(2,1)} %param.13) | copy-start | bytes 27652
  12.3 5.4 %copy-start.1 = (bf16[12,48,48]{2,1,0:T(8,128)(2,1)S(1)}, bf16[12,48,48]{2,1,0:T(8,128)(2,1)}, u32[]{:S(2)}) copy-start(bf16[12,48,48]{2,1,0:T(8,128)(2,1)} %param.11) | copy-start | bytes 165892
  16.7 0.7 copy-start.5
  17.7 6.9 %collective-permute-start.3 = (bf16[4,48,48]{2,1,0:T(8,128)(2,1)S(1)}, bf16[4,48,48]{2,1,0:T(8,128)(2,1)S(1)}, u32[]{:S(2)}, u32[]{:S(2)}) collective-permute-start(bf16[4,48,48]{2,1,0:T(8,128)(2,1)S(1)} %get-tuple-element.31), channel_id=1, source_target_pairs={{0,2},{2,4},{4,6},{6,8},{8,10},{10,12},{12,14},{1,3},{3,5},{5,7},{... | collective-permute-start | bytes 55304 | tf_op jit(solution)/shard_map/ppermute | solution.py:18
  22.9 6.0 %collective-permute-start.4 = (bf16[4,48,48]{2,1,0:T(8,128)(2,1)S(1)}, bf16[4,48,48]{2,1,0:T(8,128)(2,1)S(1)}, u32[]{:S(2)}, u32[]{:S(2)}) collective-permute-start(bf16[4,48,48]{2,1,0:T(8,128)(2,1)S(1)} %get-tuple-element.32), channel_id=1, source_target_pairs={{2,0},{4,2},{6,4},{8,6},{10,8},{12,10},{14,12},{3,1},{5,3},{7,5},{... | collective-permute-start | bytes 55304 | tf_op jit(solution)/shard_map/ppermute | solution.py:19
  28.9 2.6 %collective-permute-start.5 = (bf16[20,4,48]{2,1,0:T(4,128)(2,1)S(1)}, bf16[20,4,48]{2,1,0:T(4,128)(2,1)S(1)}, u32[]{:S(2)}, u32[]{:S(2)}) collective-permute-start(bf16[20,4,48]{2,1,0:T(4,128)(2,1)S(1)} %get-tuple-element.25), channel_id=1, source_target_pairs={{0,1},{2,3},{4,5},{6,7},{8,9},{10,11},{12,13},{14,15},{16,17},{18,... | collective-permute-start | bytes 23048 | tf_op jit(solution)/shard_map/ppermute | solution.py:18
  30.2 3.1 %collective-permute-start.6 = (bf16[20,4,48]{2,1,0:T(4,128)(2,1)S(1)}, bf16[20,4,48]{2,1,0:T(4,128)(2,1)S(1)}, u32[]{:S(2)}, u32[]{:S(2)}) collective-permute-start(bf16[20,4,48]{2,1,0:T(4,128)(2,1)S(1)} %get-tuple-element.26), channel_id=1, source_target_pairs={{1,0},{3,2},{5,4},{7,6},{9,8},{11,10},{13,12},{15,14},{17,16},{19,... | collective-permute-start | bytes 23048 | tf_op jit(solution)/shard_map/ppermute | solution.py:19
  34.3 0.7 copy-start.6
  35.3 5.5 %collective-permute-start.7 = (bf16[8,48,48]{2,1,0:T(8,128)(2,1)S(1)}, bf16[8,48,48]{2,1,0:T(8,128)(2,1)S(1)}, u32[]{:S(2)}, u32[]{:S(2)}) collective-permute-start(bf16[8,48,48]{2,1,0:T(8,128)(2,1)S(1)} %get-tuple-element.29), channel_id=1, source_target_pairs={{0,2},{2,4},{4,6},{6,8},{8,10},{10,12},{12,14},{1,3},{3,5},{5,7},{... | collective-permute-start | bytes 110600 | tf_op jit(solution)/shard_map/ppermute | solution.py:18
  38.4 6.8 %collective-permute-start.8 = (bf16[8,48,48]{2,1,0:T(8,128)(2,1)S(1)}, bf16[8,48,48]{2,1,0:T(8,128)(2,1)S(1)}, u32[]{:S(2)}, u32[]{:S(2)}) collective-permute-start(bf16[8,48,48]{2,1,0:T(8,128)(2,1)S(1)} %get-tuple-element.30), channel_id=1, source_target_pairs={{2,0},{4,2},{6,4},{8,6},{10,8},{12,10},{14,12},{3,1},{5,3},{7,5},{... | collective-permute-start | bytes 110600 | tf_op jit(solution)/shard_map/ppermute | solution.py:19
  45.1 4.3 %collective-permute-start.10 = (bf16[28,8,48]{2,1,0:T(8,128)(2,1)S(1)}, bf16[28,8,48]{2,1,0:T(8,128)(2,1)S(1)}, u32[]{:S(2)}, u32[]{:S(2)}) collective-permute-start(bf16[28,8,48]{2,1,0:T(8,128)(2,1)S(1)} %get-tuple-element.15), channel_id=1, source_target_pairs={{1,0},{3,2},{5,4},{7,6},{9,8},{11,10},{13,12},{15,14},{17,16},{19,... | collective-permute-start | bytes 64520 | tf_op jit(solution)/shard_map/ppermute | solution.py:19
  46.4 3.9 %collective-permute-start.9 = (bf16[28,8,48]{2,1,0:T(8,128)(2,1)S(1)}, bf16[28,8,48]{2,1,0:T(8,128)(2,1)S(1)}, u32[]{:S(2)}, u32[]{:S(2)}) collective-permute-start(bf16[28,8,48]{2,1,0:T(8,128)(2,1)S(1)} %get-tuple-element.14), channel_id=1, source_target_pairs={{0,1},{2,3},{4,5},{6,7},{8,9},{10,11},{12,13},{14,15},{16,17},{18,... | collective-permute-start | bytes 64520 | tf_op jit(solution)/shard_map/ppermute | solution.py:18
  50.7 0.9 %copy-start.2 = (bf16[3,3,48,48]{3,2,1,0:T(8,128)(2,1)S(1)}, bf16[3,3,48,48]{3,2,1,0:T(8,128)(2,1)}, u32[]{:S(2)}) copy-start(bf16[3,3,48,48]{3,2,1,0:T(8,128)(2,1)} %param.17) | copy-start | bytes 124420
  51.4 0.7 copy-start.7
  53.3 13.1 %all-to-all-start = ((bf16[8,2,1728]{2,1,0:T(2,128)(2,1)}), bf16[8,2,1728]{2,1,0:T(2,128)(2,1)S(1)}, u32[]{:S(2)}, u32[]{:S(2)}) async-start(bf16[8,2,1728]{2,1,0:T(2,128)(2,1)} %reshape.33), calls=%async_computation | async-start | bytes 114688 | tf_op jit(solution)/shard_map/all_to_all | solution.py:116
  71.1 6.6 %collective-permute-start.11 = (bf16[4,6,12,48]{3,0,2,1:T(4,128)(2,1)S(1)}, bf16[4,6,12,48]{3,0,2,1:T(4,128)(2,1)S(1)}, u32[]{:S(2)}, u32[]{:S(2)}) collective-permute-start(bf16[4,6,12,48]{3,0,2,1:T(4,128)(2,1)S(1)} %get-tuple-element.28), channel_id=1, source_target_pairs={{0,8},{2,10},{4,12},{6,14},{8,0},{10,2},{12,4},{14,6},{1,9},{3,11}... | collective-permute-start | bytes 82952 | tf_op jit(solution)/shard_map/ppermute | solution.py:27
  78.0 0.7 copy-start.8
  78.1 0.7 copy-start.9
  78.1 0.7 copy-start.10
